TPU v7x, 32 devices: a whole 2x2x4 slice. The times are simulated.
32 devices in a mesh: groups: 2 (over x), views: 16 (over z, y, core).
Axes of the slice: x: 2, y: 2, z: 4, core: 2. Of those that a mesh axis runs over, the one named last changes fastest.
Arguments:
- source_rows: bfloat16 [384, 320, 128], P(('groups', 'views')), parts along dimension 0, may hold values from -6 to 6
- route_owner: int32 [384, 1], P(('groups', 'views')), parts along dimension 0, may hold values from 0 to 15; in each aligned block of 12 rows (0 to 11, 12 to 23, ...) at most 2 rows name the same one
- target_row: int32 [384], P(('groups', 'views')), parts along dimension 0, may hold values from 0 to 3
- start_index: int32 [384], P(('groups', 'views')), parts along dimension 0, may hold values from 0 to 15
- reference_rows: bfloat16 [128, 320, 128], P(('groups', 'views')), parts along dimension 0, may hold values from -96 to 96
- conv_weight: float32 [40, 3, 3, 3], replicated, may hold values from -3 to 3
Outputs:
- depth_map: float32 [128, 128], P(('groups', 'views')), parts along dimension 0
There are 2 independent parts, one for each index of `groups`. A program takes and returns all parts, laid end to end along the dimension named above; an argument that names none is the same for every part. Nothing has to cross between parts.
Inputs may be any that keep to these rules, and one draw needn't show every extreme that they name: `route_owner`: among the rows of one device, no owner is named more than 2 times, a bound that some block reaches.
All inputs are finite; a program needn't handle non-finite values.
Results may differ from a plain program's by a relative error of at most 0.0003.
Values may be sent and summed in bfloat16 or wider, within the bound.
No kernel may reach another device: no remote copies, remote signals or barrier semaphores. Data moves between devices by JAX's collectives and lax.ppermute only.
A program may use at most 128 MiB of HBM per device.

v0:
```python
import math

import jax
import jax.numpy as jnp
from jax import lax
from jax.sharding import PartitionSpec as P

C = 320
G = 40
CG = 8
DISP = 96
TW = 128
DSPAN = 16
CAP = 2


def with_halo(cells, sides, width):
    for axis, dim in sides:
        count = lax.axis_size(axis)
        ends = count - 1
        head = lax.slice_in_dim(cells, 0, width, axis=dim)
        tail = lax.slice_in_dim(cells, cells.shape[dim] - width, cells.shape[dim], axis=dim)
        cells = jnp.concatenate(
            [
                lax.ppermute(tail, axis, [(i, (i + 1) % count) for i in range(ends)]),
                cells,
                lax.ppermute(head, axis, [((i + 1) % count, i) for i in range(ends)]),
            ],
            axis=dim,
        )
    return cells


def cost_rows(reference_part, canvas_part):
    row_count = reference_part.shape[0]
    left_side = reference_part.reshape(row_count, G, CG, TW)
    right_side = canvas_part.reshape(row_count, G, CG, 2 * TW)
    level_list = []
    for level in range(DISP):
        first = DISP - 1 - level
        level_list.append(jnp.sum(left_side * right_side[:, :, :, first : first + TW], axis=2))
    return jnp.stack(level_list, axis=2) / CG


def shift_along(values, axis_number, offset):
    if offset == 0:
        return values
    length = values.shape[axis_number]
    zero_shape = list(values.shape)
    zero_shape[axis_number] = 1
    zeros_part = jnp.zeros(tuple(zero_shape), values.dtype)
    if offset > 0:
        kept = lax.slice_in_dim(values, 1, length, 1, axis_number)
        return jnp.concatenate([kept, zeros_part], axis=axis_number)
    kept = lax.slice_in_dim(values, 0, length - 1, 1, axis_number)
    return jnp.concatenate([zeros_part, kept], axis=axis_number)


def body(source_rows, route_owner, target_row, start_index, reference_rows, conv_weight):
    owners = lax.axis_size("views")
    total_slots = owners * CAP
    item_count = source_rows.shape[0]
    owner_dest = route_owner[:, 0]
    owner_onehot = (owner_dest[:, None] == jnp.arange(owners, dtype=jnp.int32)[None, :]).astype(
        jnp.int32
    )
    earlier = jnp.cumsum(owner_onehot, axis=0) - owner_onehot
    position = jnp.sum(earlier * owner_onehot, axis=1)
    slot_of = owner_dest * CAP + position
    inverse = (
        jnp.full((total_slots,), -1, jnp.int32)
        .at[slot_of]
        .set(jnp.arange(item_count, dtype=jnp.int32))
    )
    filled = inverse >= 0
    picked = jnp.maximum(inverse, 0)
    outgoing = jnp.where(
        filled[:, None, None], jnp.take(source_rows, picked, axis=0), jnp.zeros((), jnp.bfloat16)
    )
    sent_row = jnp.where(filled, jnp.take(target_row, picked), -1)
    sent_start = jnp.where(filled, jnp.take(start_index, picked), 0)
    sent_meta = jnp.stack([sent_row, sent_start], axis=1)
    arrived, arrived_meta = (
        lax.all_to_all(outgoing, "views", split_axis=0, concat_axis=0, tiled=True),
        lax.all_to_all(sent_meta, "views", split_axis=0, concat_axis=0, tiled=True),
    )
    local_rows = reference_rows.shape[0]
    rows_in = arrived_meta[:, 0]
    starts_in = arrived_meta[:, 1]
    assign = jnp.arange(local_rows, dtype=jnp.int32)[:, None] == rows_in[None, :]
    pair_count = jnp.sum(assign.astype(jnp.float32), axis=1)
    bucket_count = local_rows * DSPAN
    bucket_id = jnp.where(rows_in >= 0, rows_in * DSPAN + starts_in, bucket_count).astype(jnp.int32)
    block_size = math.gcd(total_slots, 32)

    def add_block(block_index, accumulated):
        first = block_index * block_size
        block_rows = lax.dynamic_slice_in_dim(arrived, first, block_size, 0).astype(jnp.float32)
        block_ids = lax.dynamic_slice_in_dim(bucket_id, first, block_size, 0)
        return accumulated + jax.ops.segment_sum(block_rows, block_ids, num_segments=bucket_count)

    grouped_flat = lax.fori_loop(
        0, total_slots // block_size, add_block, jnp.zeros((bucket_count, C, TW), jnp.float32)
    )
    grouped = grouped_flat.reshape(local_rows, DSPAN, C, TW)
    canvas = jnp.zeros((local_rows, C, 2 * TW), jnp.float32)
    for start_value in range(DSPAN):
        canvas = canvas + jnp.pad(
            grouped[:, start_value],
            ((0, 0), (0, 0), (DISP - 1 + start_value, TW - DISP + 1 - start_value)),
        )
    mean_canvas = canvas / jnp.maximum(pair_count, 1.0)[:, None, None]
    reference_wide = reference_rows.astype(jnp.float32)
    own_volume = cost_rows(reference_wide, mean_canvas)
    volume = with_halo(own_volume, (("views", 0),), 1)
    taps_all = jnp.einsum(
        "rgkx,gt->trkx", volume, conv_weight.reshape(G, 27), precision=lax.Precision.HIGHEST
    )
    scores = jnp.zeros((local_rows, DISP, TW), jnp.float32)
    for shift_pixel in range(3):
        partial_sum = jnp.zeros((local_rows, DISP, TW), jnp.float32)
        for shift_row in range(3):
            for shift_level in range(3):
                tap_index = 9 * shift_row + 3 * shift_level + shift_pixel
                tap_rows = taps_all[tap_index, shift_row : shift_row + local_rows]
                partial_sum = partial_sum + shift_along(tap_rows, 1, shift_level - 1)
        scores = scores + shift_along(partial_sum, 2, shift_pixel - 1)
    weights = jax.nn.softmax(scores, axis=1)
    levels = jnp.arange(DISP, dtype=jnp.float32) / DISP
    return jnp.sum(weights * levels[None, :, None], axis=1)


def solution(mesh):
    in_specs = (
        P(("groups", "views"), None, None),
        P(("groups", "views"), None),
        P(("groups", "views")),
        P(("groups", "views")),
        P(("groups", "views"), None, None),
        P(),
    )
    out_specs = P(("groups", "views"), None)
    return jax.shard_map(body, mesh=mesh, in_specs=in_specs, out_specs=out_specs, check_vma=False)
```

profile of v0, /device:TPU:17, one launch (start us, length us, event | category | flops | bytes accessed | tf_op | source)
XLA Modules:
  0.0 212.3 jit_solution(12183827195400364415)
XLA Ops:
  0.0 0.8 fusion.112
  0.8 0.8 select_reduce_fusion
  1.7 0.7 fusion.114
  3.0 1.4 gather_fusion.1
  4.3 1.4 gather_fusion.2
  5.9 0.6 copy.119
  6.5 6.5 %all-to-all-start = ((s32[16,2,2]{1,2,0:T(2,128)}), s32[16,2,2]{1,2,0:T(2,128)S(1)}, u32[]{:S(2)}, u32[]{:S(2)}) async-start(s32[16,2,2]{1,2,0:T(2,128)} %copy.119), calls=%async_computation | async-start | bytes 32768 | tf_op jit(solution)/shard_map/all_to_all | solution.py:85
  13.0 2.4 %gather_fusion = bf16[32,320,128]{2,1,0:T(8,128)(2,1)} fusion(bf16[12,320,128]{2,1,0:T(8,128)(2,1)S(1)} %copy-done, s32[1024]{0:T(1024)S(1)} %pad_clamp_fusion), kind=kCustom, calls=%fused_computation.2 | custom fusion | bytes 5243008 | tf_op jit(solution)/shard_map/jit(_take)/gather | solution.py:78
  15.4 3.7 %select_select_fusion = bf16[32,320,128]{2,1,0:T(8,128)(2,1)} fusion(bf16[32,320,128]{2,1,0:T(8,128)(2,1)} %gather_fusion, pred[32]{0:T(512)(128)(4,1)S(1)} %get-tuple-element.165, pred[32]{0:T(512)(128)(4,1)S(1)} %get-tuple-element.164), kind=kLoop, calls=%fused_computation.111 | loop fusion | flops 2621440 | bytes 5242944 | tf_op jit(solution)/shard_map/jit(_where)/select_n | solution.py:77
  19.1 6.0 %all-to-all-start.1 = ((bf16[32,320,128]{2,1,0:T(8,128)(2,1)}), bf16[32,320,128]{2,1,0:T(8,128)(2,1)}, u32[]{:S(2)}, u32[]{:S(2)}) async-start(bf16[32,320,128]{2,1,0:T(8,128)(2,1)} %select_select_fusion), calls=%async_computation.1 | async-start | bytes 5242880 | tf_op jit(solution)/shard_map/all_to_all | solution.py:84
  25.4 58.1 %all-to-all-done.1 = bf16[32,320,128]{2,1,0:T(8,128)(2,1)} async-done(((bf16[32,320,128]{2,1,0:T(8,128)(2,1)}), bf16[32,320,128]{2,1,0:T(8,128)(2,1)}, u32[]{:S(2)}, u32[]{:S(2)}) %all-to-all-start.1) | async-done | bytes 2621472 | tf_op jit(solution)/shard_map/all_to_all | solution.py:84
  83.5 4.7 %convert_element_type.44 = f32[32,320,128]{2,1,0:T(8,128)} convert(bf16[32,320,128]{2,1,0:T(8,128)(2,1)} %all-to-all-done.1) | non-fusion elementwise | flops 1310720 | bytes 7864320 | tf_op jit(solution)/shard_map/while/body/eval_jaxpr/convert_element_type | solution.py:98
  88.2 5.3 %broadcast.125 = f32[64,320,128]{2,1,0:T(8,128)} broadcast(f32[]{:T(128)} %constant.24.clone.1), dimensions={} | broadcast | bytes 10485764 | tf_op jit(solution)/shard_map/broadcast.13
  93.5 11.4 %scatter_fusion = f32[64,320,128]{2,1,0:T(8,128)} fusion(f32[64,320,128]{2,1,0:T(8,128)} %broadcast.125, s32[32]{0:T(128)S(1)} %get-tuple-element.163, f32[32,320,128]{2,1,0:T(8,128)} %convert_element_type.44), kind=kCustom, calls=%fused_computation.4 | custom fusion | flops 1310720 | bytes 15728768 | tf_op jit(solution)/shard_map/while/body/eval_jaxpr/scatter-add | solution.py:100
  104.9 4.8 %slice_bitcast_fusion.15 = (f32[4,320,128]{2,1,0:T(8,128)S(1)}, f32[4,320,128]{2,1,0:T(8,128)S(1)}, f32[4,320,128]{2,1,0:T(8,128)S(1)}, f32[4,320,128]{2,1,0:T(8...) fusion(f32[4,16,320,128]{3,2,1,0:T(8,128)} %bitcast.463), kind=kLoop, calls=%fused_computation.228 | loop fusion | bytes 20971520 | tf_op jit(solution)/shard_map/squeeze | solution.py:109
  109.6 5.6 %divide_bitcast_fusion = f32[4,40,8,256]{3,2,1,0:T(8,128)S(1)} fusion(f32[4,320,128]{2,1,0:T(8,128)S(1)} %get-tuple-element.131, f32[4,320,128]{2,1,0:T(8,128)S(1)} %get-tuple-element.132, f32[4,320,128]{2,1,0:T(8,128)S(1)} %get-tuple-element.118, f32[4,320,128]{2,1,0:T(8,128)S(1)} %get-tuple-element.119, f32[4,320,128]{2,1,0:T(8,128)S(1)} %get-tuple-element.120, ...), kind=kLoop, calls=%fused_computation.112 | loop fusion | flops 5242880 | bytes 11796496 | tf_op jit(solution)/shard_map/reshape | solution.py:37
  115.2 1.2 fusion.20
  116.5 4.4 %fusion.38 = (f32[4,40,128]{2,1,0:T(8,128)S(1)}, f32[4,40,128]{2,1,0:T(8,128)S(1)}, f32[4,40,128]{2,1,0:T(8,128)S(1)}, f32[4,40,128]{2,1,0:T(8,128)S(1)}, f32[4,...) fusion(f32[4,40,8,256]{3,2,1,0:T(8,128)S(1)} %divide_bitcast_fu, ...), kind=kLoop, calls=%fused_computation.140 | loop fusion | flops 5693440 | bytes 13598720 | tf_op jit(solution)/shard_map/reduce_sum | solution.py:41
  120.9 4.5 %fusion.56 = (f32[4,40,128]{2,1,0:T(8,128)S(1)}, f32[4,40,128]{2,1,0:T(8,128)S(1)}, f32[4,40,128]{2,1,0:T(8,128)S(1)}, f32[4,40,128]{2,1,0:T(8,128)S(1)}, f32[4,...) fusion(f32[4,40,8,256]{3,2,1,0:T(8,128)S(1)} %divide_bitcast_fu, ...), kind=kLoop, calls=%fused_computation.158 | loop fusion | flops 5693440 | bytes 13598720 | tf_op jit(solution)/shard_map/reduce_sum | solution.py:41
  125.4 4.4 %fusion.74 = (f32[4,40,128]{2,1,0:T(8,128)S(1)}, f32[4,40,128]{2,1,0:T(8,128)S(1)}, f32[4,40,128]{2,1,0:T(8,128)S(1)}, f32[4,40,128]{2,1,0:T(8,128)S(1)}, f32[4,...) fusion(f32[4,40,8,256]{3,2,1,0:T(8,128)S(1)} %divide_bitcast_fu, ...), kind=kLoop, calls=%fused_computation.176 | loop fusion | flops 5693440 | bytes 13598720 | tf_op jit(solution)/shard_map/reduce_sum | solution.py:41
  129.8 4.4 %fusion.92 = (f32[4,40,128]{2,1,0:T(8,128)S(1)}, f32[4,40,128]{2,1,0:T(8,128)S(1)}, f32[4,40,128]{2,1,0:T(8,128)S(1)}, f32[4,40,128]{2,1,0:T(8,128)S(1)}, f32[4,...) fusion(f32[4,40,8,256]{3,2,1,0:T(8,128)S(1)} %divide_bitcast_fu, ...), kind=kLoop, calls=%fused_computation.194 | loop fusion | flops 5693440 | bytes 13598720 | tf_op jit(solution)/shard_map/reduce_sum | solution.py:41
  134.2 4.2 %fusion.110 = (f32[4,40,128]{2,1,0:T(8,128)S(1)}, f32[4,40,128]{2,1,0:T(8,128)S(1)}, f32[4,40,128]{2,1,0:T(8,128)S(1)}, f32[4,40,128]{2,1,0:T(8,128)S(1)}, f32[4...) fusion(f32[4,40,8,256]{3,2,1,0:T(8,128)S(1)} %divide_bitcast_fu, ...), kind=kLoop, calls=%fused_computation.212 | loop fusion | flops 5693440 | bytes 13598720 | tf_op jit(solution)/shard_map/reduce_sum | solution.py:41
  140.5 3.1 %copy-done.2 = f32[4,40,96,128]{3,1,2,0:T(8,128)} copy-done((f32[4,40,96,128]{3,1,2,0:T(8,128)}, f32[4,40,96,128]{3,1,2,0:T(8,128)S(1)}, u32[]{:S(2)}) %copy-start.2) | copy-done | bytes 7864344
  143.6 2.2 %fusion.121 = (f32[1,40,96,128]{3,1,2,0:T(8,128)}, f32[1,40,96,128]{3,1,2,0:T(8,128)}) fusion(f32[4,40,96,128]{3,1,2,0:T(8,128)S(1)} %broadcast_multiply_fusion), kind=kLoop, calls=%fused_computation.367 | loop fusion | bytes 7864320 | tf_op jit(solution)/shard_map/slice | solution.py:22
  145.8 2.0 collective-permute-start
  147.8 2.6 %collective-permute-start.1 = (f32[1,40,96,128]{3,1,2,0:T(8,128)}, f32[1,40,96,128]{3,1,2,0:T(8,128)}, u32[]{:S(2)}, u32[]{:S(2)}) collective-permute-start(f32[1,40,96,128]{3,1,2,0:T(8,128)} %get-tuple-element.161), channel_id=1, source_target_pairs={{1,0},{2,1},{3,2},{4,3},{5,4},{6,5},{7,6},{8,7},{9,8},{10,9},{11,1... | collective-permute-start | bytes 5898248 | tf_op jit(solution)/shard_map/ppermute | solution.py:27
  150.5 40.3 %collective-permute-done = f32[1,40,96,128]{3,1,2,0:T(8,128)S(1)} collective-permute-done((f32[1,40,96,128]{3,1,2,0:T(8,128)}, f32[1,40,96,128]{3,1,2,0:T(8,128)S(1)}, u32[]{:S(2)}, u32[]{:S(2)}) %collective-permute-start) | collective-permute-done | bytes 1966112 | tf_op jit(solution)/shard_map/ppermute | solution.py:25
  190.8 3.4 %collective-permute-done.1 = f32[1,40,96,128]{3,1,2,0:T(8,128)} collective-permute-done((f32[1,40,96,128]{3,1,2,0:T(8,128)}, f32[1,40,96,128]{3,1,2,0:T(8,128)}, u32[]{:S(2)}, u32[]{:S(2)}) %collective-permute-start.1) | collective-permute-done | bytes 1966112 | tf_op jit(solution)/shard_map/ppermute | solution.py:27
  194.1 12.2 %fusion.8 = f32[27,6,96,128]{3,0,2,1:T(8,128)S(1)} fusion(f32[1,40,96,128]{3,1,2,0:T(8,128)} %collective-permute-done.1, f32[4,40,96,128]{3,1,2,0:T(8,128)} %copy-done.2, f32[1,40,96,128]{3,1,2,0:T(8,128)S(1)} %collective-permute-done, f32[40,27,1,1]{0,1,2,3:T(8,128)S(1)} %reshape.97), kind=kOutput, calls=%fused_computation.110 | convolution fusion | flops 961413120 | bytes 19763424 | tf_op jit(solution)/shard_map/rgkx,gt->trkx/dot_general | solution.py:116
  206.4 2.6 %fusion.119 = (f32[1,4,96,128]{3,0,2,1:T(1,128)S(1)}, f32[1,4,96,128]{3,0,2,1:T(1,128)S(1)}, f32[1,4,96,128]{3,0,2,1:T(1,128)S(1)}, f32[1,4,96,128]{3,0,2,1:T(1,...) fusion(f32[27,6,96,128]{3,0,2,1:T(8,128)S(1)} %fusion.8), kind=kLoop, calls=%fused_computation.365 | loop fusion | bytes 7471104 | tf_op jit(solution)/shard_map/slice | solution.py:125
  209.0 1.7 fusion.120
  211.5 0.8 fusion.122
  (136 shorter events, 3.1 us)
Async XLA Ops:
  0.0 13.0 %copy-start = (bf16[12,320,128]{2,1,0:T(8,128)(2,1)S(1)}, bf16[12,320,128]{2,1,0:T(8,128)(2,1)}, u32[]{:S(2)}) copy-start(bf16[12,320,128]{2,1,0:T(8,128)(2,1)} %param.8) | copy-start | bytes 2949124
  6.5 12.6 %all-to-all-start = ((s32[16,2,2]{1,2,0:T(2,128)}), s32[16,2,2]{1,2,0:T(2,128)S(1)}, u32[]{:S(2)}, u32[]{:S(2)}) async-start(s32[16,2,2]{1,2,0:T(2,128)} %copy.119), calls=%async_computation | async-start | bytes 32768 | tf_op jit(solution)/shard_map/all_to_all | solution.py:85
  19.1 64.4 %all-to-all-start.1 = ((bf16[32,320,128]{2,1,0:T(8,128)(2,1)}), bf16[32,320,128]{2,1,0:T(8,128)(2,1)}, u32[]{:S(2)}, u32[]{:S(2)}) async-start(bf16[32,320,128]{2,1,0:T(8,128)(2,1)} %select_select_fusion), calls=%async_computation.1 | async-start | bytes 5242880 | tf_op jit(solution)/shard_map/all_to_all | solution.py:84
  109.6 5.6 %copy-start.3 = (bf16[4,320,128]{2,1,0:T(8,128)(2,1)S(1)}, bf16[4,320,128]{2,1,0:T(8,128)(2,1)}, u32[]{:S(2)}) copy-start(bf16[4,320,128]{2,1,0:T(8,128)(2,1)} %param.12) | copy-start | bytes 983044
  140.5 3.1 %copy-start.2 = (f32[4,40,96,128]{3,1,2,0:T(8,128)}, f32[4,40,96,128]{3,1,2,0:T(8,128)S(1)}, u32[]{:S(2)}) copy-start(f32[4,40,96,128]{3,1,2,0:T(8,128)S(1)} %broadcast_multiply_fusion) | copy-start | bytes 23592964
  143.6 6.9 %copy-start.4 = (f32[40,3,3,3]{0,3,2,1:T(4,128)S(1)}, f32[40,3,3,3]{0,3,2,1:T(4,128)}, u32[]{:S(2)}) copy-start(f32[40,3,3,3]{0,3,2,1:T(4,128)} %param.13) | copy-start | bytes 12964
  145.8 44.9 %collective-permute-start = (f32[1,40,96,128]{3,1,2,0:T(8,128)}, f32[1,40,96,128]{3,1,2,0:T(8,128)S(1)}, u32[]{:S(2)}, u32[]{:S(2)}) collective-permute-start(f32[1,40,96,128]{3,1,2,0:T(8,128)} %get-tuple-element.160), channel_id=1, source_target_pairs={{0,1},{1,2},{2,3},{3,4},{4,5},{5,6},{6,7},{7,8},{8,9},{9,10},{10,1... | collective-permute-start | bytes 5898248 | tf_op jit(solution)/shard_map/ppermute | solution.py:25
  147.8 46.3 %collective-permute-start.1 = (f32[1,40,96,128]{3,1,2,0:T(8,128)}, f32[1,40,96,128]{3,1,2,0:T(8,128)}, u32[]{:S(2)}, u32[]{:S(2)}) collective-permute-start(f32[1,40,96,128]{3,1,2,0:T(8,128)} %get-tuple-element.161), channel_id=1, source_target_pairs={{1,0},{2,1},{3,2},{4,3},{5,4},{6,5},{7,6},{8,7},{9,8},{10,9},{11,1... | collective-permute-start | bytes 5898248 | tf_op jit(solution)/shard_map/ppermute | solution.py:27
  206.4 6.0 %copy-start.1 = (bf16[12,320,128]{2,1,0:T(8,128)(2,1)S(1)}, bf16[12,320,128]{2,1,0:T(8,128)(2,1)}, u32[]{:S(2)}) copy-start(bf16[12,320,128]{2,1,0:T(8,128)(2,1)} %param.8) | copy-start | bytes 2949124
where the time goes:
time: 213 us; the launch traced here: 212 us
  waiting for transfers between devices  102 us (48%)
  other arithmetic  52.9 us (25%)
  local copies, waits for them, and re-layouts  27.3 us (13%)
  starting transfers between devices  17.1 us (8%)
  matrix products  12.2 us (6%)
    all_to_all x1, waiting for transfers between devices, body(): lax.all_to_all(outgoing, 'views', split_axis=0, concat_axis=0, tiled=True)  58.1 us
    ppermute x1, waiting for transfers between devices, with_halo(): lax.ppermute(tail, axis, [(i, (i + 1) % count) for i in range(ends)])  40.3 us
    reduce_sum x6, other arithmetic, cost_rows(): jnp.sum(left_side * right_side[:, :, :, first:first + TW], axis=2)  23.1 us
    dot_general x1, matrix products, body(): jnp.einsum('rgkx,gt->trkx', volume, conv_weight.reshape(G, 27), precision...  12.2 us
    scatter-add x1, other arithmetic, add_block(): jax.ops.segment_sum(block_rows, block_ids, num_segments=bucket_count)  11.4 us
    all_to_all x1, starting transfers between devices, body(): lax.all_to_all(sent_meta, 'views', split_axis=0, concat_axis=0, tiled=True)  6.47 us
    all_to_all x1, starting transfers between devices, body(): lax.all_to_all(outgoing, 'views', split_axis=0, concat_axis=0, tiled=True)  6.02 us
    reshape x1, other arithmetic, cost_rows(): right_side = canvas_part.reshape(row_count, G, CG, 2 * TW)  5.6 us
  transfers between devices with their start and end apart: 4, of which 3 were waited for; matrix products, arithmetic and copies ran while one was open for 3% of the time, Pallas kernels for 0%

commit v1 on v0

v1 whole, which is shorter than its diff:
```python
import functools

import jax
import jax.numpy as jnp
from jax import lax
from jax.experimental import pallas as pl
from jax.experimental.pallas import tpu as pltpu
from jax.sharding import PartitionSpec as P

CG = 8
DISP = 96
DSPAN = 16
CAP = 2
CHUNKS = 4

VMEM = pl.BlockSpec(memory_space=pltpu.VMEM)
SMEM = pl.BlockSpec(memory_space=pltpu.SMEM)
ANY = pl.BlockSpec(memory_space=pl.ANY)


def pack_kernel(parts, route_ref, target_ref, start_ref, source_ref, *rest):
    outs, meta_ref, count_ref, sem = rest[:parts], rest[parts], rest[parts + 1], rest[parts + 2]
    items, channels = source_ref.shape[0], source_ref.shape[1]
    slots = meta_ref.shape[0]
    width = channels // parts

    @pl.loop(0, slots)
    def _(s):
        meta_ref[s] = -1

    @pl.loop(0, slots // CAP)
    def _(s):
        count_ref[s] = 0

    @pl.loop(0, items)
    def _(i):
        owner = route_ref[i, 0]
        slot = owner * CAP + count_ref[owner]
        count_ref[owner] = count_ref[owner] + 1
        meta_ref[slot] = target_ref[i] * DSPAN + start_ref[i]
        for p in range(parts):
            pltpu.make_async_copy(
                source_ref.at[i, pl.ds(p * width, width), :], outs[p].at[slot], sem
            ).start()

    @pl.loop(0, items)
    def _(i):
        for p in range(parts):
            pltpu.make_async_copy(
                source_ref.at[0, pl.ds(p * width, width), :], outs[p].at[0], sem
            ).wait()


def pack_rows(route, target, start, source, slots, parts):
    items, channels, pixels = source.shape
    width = channels // parts
    return pl.pallas_call(
        functools.partial(pack_kernel, parts),
        out_shape=[jax.ShapeDtypeStruct((slots, width, pixels), source.dtype)] * parts
        + [jax.ShapeDtypeStruct((slots,), jnp.int32)],
        in_specs=[SMEM, SMEM, SMEM, VMEM],
        out_specs=[ANY] * parts + [SMEM],
        scratch_shapes=[pltpu.SMEM((slots // CAP,), jnp.int32), pltpu.SemaphoreType.DMA],
        name="pack_rows",
    )(route, target, start, source)


def split_two(values):
    high = values.astype(jnp.bfloat16)
    return high, (values - high.astype(jnp.float32)).astype(jnp.bfloat16)


def shift_left(values, offset):
    lane = lax.broadcasted_iota(jnp.int32, values.shape, 1)
    pixels = values.shape[1]
    moved = pltpu.roll(values, (-offset) % pixels, 1)
    return jnp.where((lane + offset >= 0) & (lane + offset < pixels), moved, 0.0)


def chunk_kernel(first, last, meta_ref, arrived_ref, left_ref, weight_ref, edge_ref, *rest):
    if first:
        total_ref, canvas_ref = rest
        total_ref[...] = jnp.zeros_like(total_ref)
    elif last:
        before_ref, out_ref, canvas_ref, total_ref = rest
        total_ref[...] = before_ref[...]
    else:
        before_ref, total_ref, canvas_ref = rest
        total_ref[...] = before_ref[...]
    slots, width, pixels = arrived_ref.shape
    rows = canvas_ref.shape[0]
    canvas_ref[...] = jnp.zeros_like(canvas_ref)
    lane = lax.broadcasted_iota(jnp.int32, (width, pixels), 1)

    def add_slot(s, counts):
        code = meta_ref[s]
        row = code // DSPAN
        begin = code % DSPAN

        @pl.when(code >= 0)
        def _():
            moved = pltpu.roll(arrived_ref[s].astype(jnp.float32), begin, 1)
            canvas_ref[row] = canvas_ref[row] + jnp.where(lane >= begin, moved, 0.0)

        return tuple(
            count + jnp.where((code >= 0) & (row == r), 1, 0) for r, count in enumerate(counts)
        )

    counts = lax.fori_loop(0, slots, add_slot, (jnp.int32(0),) * rows)

    @pl.loop(0, rows)
    def _(r):
        count = counts[0]
        for other in range(1, rows):
            count = jnp.where(r == other, counts[other], count)
        mean = canvas_ref[r] / jnp.full(
            (width, pixels), jnp.maximum(count, 1).astype(jnp.float32)
        )
        right = jnp.concatenate([shift_left(mean, e) for e in (-1, 0, 1)], axis=0)
        high, low = split_two(right)
        both = jnp.concatenate([high, low], axis=1)
        edge = jnp.broadcast_to(mean[:, :1], (width, pixels)) * edge_ref[...]
        blank = jnp.zeros((2 * width, pixels), jnp.float32)
        edge_high, edge_low = split_two(jnp.concatenate([blank, edge], axis=0))
        wide = jnp.dot(
            left_ref[r],
            jnp.concatenate([edge_high, edge_low], axis=1),
            preferred_element_type=jnp.float32,
        )
        place = (rows + 2) * 3 + r
        total_ref[place] = total_ref[place] + (wide[:, :pixels] + wide[:, pixels:])
        left = left_ref[r].astype(jnp.float32)
        for a in range(3):
            for b in range(3):
                tap = 3 * a + b
                left_high, left_low = split_two(left * weight_ref[tap : tap + 1, :])
                wide = jnp.dot(left_high, both, preferred_element_type=jnp.float32)
                part = wide[:, :pixels] + wide[:, pixels:]
                part = part + jnp.dot(left_low, high, preferred_element_type=jnp.float32)
                place = (r + 2 - a) * 3 + b
                total_ref[place] = total_ref[place] + part

    if last:
        x = lax.broadcasted_iota(jnp.int32, (pixels, pixels), 0)
        v = lax.broadcasted_iota(jnp.int32, (pixels, pixels), 1)
        inside = (x >= v) & (x - v < DISP)

        @pl.loop(0, rows + 2)
        def _(r):
            total = jnp.where(inside, total_ref[3 * r + 1], 0.0)
            for b in (0, 2):
                kept = jnp.where(inside, total_ref[3 * r + b], 0.0)
                total = total + pltpu.roll(kept, (b - 1) % pixels, 1)
            out_ref[r] = total

        border = (x < DISP - 1) & ((v >= pixels - 2) | (v < 1))
        for r in range(rows):
            edge = total_ref[(rows + 2) * 3 + r]
            for a in range(3):
                moved = pltpu.roll(edge, (-8 * a) % pixels, 1) if a else edge
                out_ref[r + 2 - a] = out_ref[r + 2 - a] + jnp.where(border, moved, 0.0)


def add_chunk(first, last, meta, arrived, left, weight, edge, before):
    slots, width, pixels = arrived.shape
    rows = left.shape[0]
    totals = ((rows + 2) * 3 + rows, pixels, pixels)
    args = [meta, arrived, left, weight, edge] + ([] if first else [before])
    shape = (rows + 2, pixels, pixels) if last else totals
    scratch = [pltpu.VMEM((rows, width, pixels), jnp.float32)]
    if last:
        scratch.append(pltpu.VMEM(totals, jnp.float32))
    flops = 2 * rows * 27 * pixels * pixels * 3 * width
    return pl.pallas_call(
        functools.partial(chunk_kernel, first, last),
        out_shape=jax.ShapeDtypeStruct(shape, jnp.float32),
        in_specs=[SMEM] + [VMEM] * (len(args) - 1),
        out_specs=VMEM,
        scratch_shapes=scratch,
        cost_estimate=pl.CostEstimate(
            flops=flops,
            bytes_accessed=2 * slots * width * pixels + 8 * totals[0] * pixels * pixels,
            transcendentals=0,
        ),
        name="add_chunk",
    )(*args)


def depth_kernel(scores_ref, before_ref, after_ref, out_ref):
    rows = out_ref.shape[0]
    pixels = out_ref.shape[1]
    v = lax.broadcasted_iota(jnp.int32, (pixels, pixels), 0)
    x = lax.broadcasted_iota(jnp.int32, (pixels, pixels), 1)
    level = jnp.where(x >= v, x - v, x - v + pixels)
    valid = level < DISP
    share = level.astype(jnp.float32) / DISP
    for r in range(rows):
        scores = scores_ref[r + 1]
        if r == 0:
            scores = scores + before_ref[0]
        if r == rows - 1:
            scores = scores + after_ref[0]
        scores = jnp.where(valid, scores.T, -jnp.inf)
        top = jnp.max(scores, axis=0, keepdims=True)
        weights = jnp.exp(scores - top)
        bottom = jnp.sum(weights, axis=0, keepdims=True)
        out_ref[r : r + 1, :] = jnp.sum(weights * share, axis=0, keepdims=True) / bottom


def depth_rows(scores, before, after):
    rows, pixels = scores.shape[0] - 2, scores.shape[1]
    return pl.pallas_call(
        depth_kernel,
        out_shape=jax.ShapeDtypeStruct((rows, pixels), jnp.float32),
        in_specs=[VMEM] * 3,
        out_specs=VMEM,
        name="depth_rows",
    )(scores, before, after)


def body(source_rows, route_owner, target_row, start_index, reference_rows, conv_weight):
    owners = lax.axis_size("views")
    slots = owners * CAP
    rows, channels, pixels = reference_rows.shape
    parts = CHUNKS
    width = channels // parts
    packed = pack_rows(route_owner, target_row, start_index, source_rows, slots, parts)
    swap = functools.partial(
        lax.all_to_all, axis_name="views", split_axis=0, concat_axis=0, tiled=True
    )
    arrived = [swap(packed[0])]
    meta = swap(packed[parts].reshape(owners, CAP)).reshape(slots)
    arrived += [swap(packed[p]) for p in range(1, parts)]

    turned = jnp.swapaxes(reference_rows, 1, 2)
    padded = jnp.pad(turned, ((0, 0), (1, 1), (0, 0)))
    taps = jnp.repeat(conv_weight.transpose(1, 2, 3, 0).reshape(9, 3, -1), CG, axis=2) / CG
    edges = jnp.pad(conv_weight[..., 2], ((0, 0), (0, 0), (0, 5))).reshape(-1, 24) / CG
    edges = jnp.repeat(jnp.roll(jnp.pad(edges, ((0, 0), (0, pixels - 24))), -2, 1), CG, axis=0)
    total = None
    for p in range(parts):
        part = slice(p * width, (p + 1) * width)
        left = jnp.concatenate([padded[:, e : e + pixels, part] for e in range(3)], axis=2)
        weight = taps[:, :, part].reshape(9, 3 * width)
        total = add_chunk(p == 0, p == parts - 1, meta, arrived[p], left, weight, edges[part], total)

    ends = owners - 1
    before = lax.ppermute(total[rows + 1 :], "views", [(i, i + 1) for i in range(ends)])
    after = lax.ppermute(total[:1], "views", [(i + 1, i) for i in range(ends)])
    return depth_rows(total, before, after)


def solution(mesh):
    in_specs = (
        P(("groups", "views"), None, None),
        P(("groups", "views"), None),
        P(("groups", "views")),
        P(("groups", "views")),
        P(("groups", "views"), None, None),
        P(),
    )
    out_specs = P(("groups", "views"), None)
    return jax.shard_map(body, mesh=mesh, in_specs=in_specs, out_specs=out_specs, check_vma=False)
```

time: 213 us -> 136 us (0.64)
  the two profiles are of different devices: /device:TPU:17 before, /device:TPU:8 now
where the time goes in v1:
time: 136 us; the launch traced here: 135 us
  blocking collectives  33.9 us (25%)
  Pallas kernels  29.7 us (22%)
  waiting for transfers between devices  29.2 us (21%)
  starting transfers between devices  26 us (19%)
  local copies, waits for them, and re-layouts  12.2 us (9%)
  other arithmetic  4.29 us (3%)
    pallas_call x4, Pallas kernels, add_chunk(): pl.pallas_call(functools.partial(chunk_kernel, first, last), out_shape=ja...  24.9 us
    all_to_all x1, blocking collectives, body(): arrived += [swap(packed[p]) for p in range(1, parts)]  22.8 us
    all_to_all x2, waiting for transfers between devices, body(): arrived += [swap(packed[p]) for p in range(1, parts)]  15.9 us
    all_to_all x1, blocking collectives, body(): meta = swap(packed[parts].reshape(owners, CAP)).reshape(slots)  11.1 us
    all_to_all x2, starting transfers between devices, body(): arrived += [swap(packed[p]) for p in range(1, parts)]  9.72 us
    ppermute x1, starting transfers between devices, body(): after = lax.ppermute(total[:1], 'views', [(i + 1, i) for i in range(ends)])  9.29 us
    all_to_all x1, waiting for transfers between devices, body(): arrived = [swap(packed[0])]  8.75 us
    all_to_all x1, starting transfers between devices, body(): arrived = [swap(packed[0])]  5.05 us
  transfers between devices with their start and end apart: 5, of which 3 were waited for; matrix products, arithmetic and copies ran while one was open for 9% of the time, Pallas kernels for 13%

profile of v1, /device:TPU:8, one launch (start us, length us, event | category | flops | bytes accessed | tf_op | source)
XLA Modules:
  0.0 135.4 jit_solution(1393728915491155061)
XLA Ops:
  0.0 1.3 copy.19.route_ref
  1.3 3.0 %pack_rows.1 = (bf16[32,80,128]{2,1,0:T(8,128)(2,1)}, bf16[32,80,128]{2,1,0:T(8,128)(2,1)}, bf16[32,80,128]{2,1,0:T(8,128)(2,1)}, bf16[32,80,128]{2,1,0:T(8,128)(2,1)}, s32[32]{0:T(128)}) custom-call(s32[12,1]{1,0:T(8,128)} %copy.19.route_ref, s32[12]{0:T(128)} %target_ref.1, s32[12]{0:T(128)} %start_ref.1, bf16[12,320,128]{2,1,0:T(8,128)(2,1)} %source_ref.1), custom_call_target="tpu_custom_call" | custom-call | tf_op jit(solution)/shard_map/pack_rows/pallas_call | solution.py:57
  4.4 0.8 all_to_all.18
  5.2 11.1 %all_to_all.29 = s32[16,1,2]{2,1,0:T(1,128)S(1)} all-to-all(s32[16,1,2]{2,1,0:T(1,128)S(1)} %bitcast.24), channel_id=1, replica_groups=mesh['groups'=2,'views'=16] {'views'}, dimensions={0} | all-to-all | bytes 256 | tf_op jit(solution)/shard_map/all_to_all | solution.py:232
  16.3 22.8 %all_to_all.30.arrived_ref = bf16[32,80,128]{2,1,0:T(8,128)(2,1)} all-to-all(bf16[32,80,128]{2,1,0:T(8,128)(2,1)} %get-tuple-element.12), channel_id=1, replica_groups=mesh['groups'=2,'views'=16] {'views'}, dimensions={0} | all-to-all | bytes 1310720 | tf_op jit(solution)/shard_map/all_to_all | solution.py:233
  39.1 4.6 %all-to-all-start.3 = ((bf16[32,80,128]{2,1,0:T(8,128)(2,1)}), bf16[32,80,128]{2,1,0:T(8,128)(2,1)S(1)}, u32[]{:S(2)}, u32[]{:S(2)}) async-start(bf16[32,80,128]{2,1,0:T(8,128)(2,1)} %get-tuple-element.13), calls=%async_computation.3 | async-start | bytes 1310720 | tf_op jit(solution)/shard_map/all_to_all | solution.py:233
  44.1 15.9 %all-to-all-done.3.arrived_ref = bf16[32,80,128]{2,1,0:T(8,128)(2,1)S(1)} async-done(((bf16[32,80,128]{2,1,0:T(8,128)(2,1)}), bf16[32,80,128]{2,1,0:T(8,128)(2,1)S(1)}, u32[]{:S(2)}, u32[]{:S(2)}) %all-to-all-start.3) | async-done | bytes 655392 | tf_op jit(solution)/shard_map/all_to_all | solution.py:233
  59.9 5.1 %all-to-all-start.4 = ((bf16[32,80,128]{2,1,0:T(8,128)(2,1)}), bf16[32,80,128]{2,1,0:T(8,128)(2,1)S(1)}, u32[]{:S(2)}, u32[]{:S(2)}) async-start(bf16[32,80,128]{2,1,0:T(8,128)(2,1)} %get-tuple-element.14), calls=%async_computation.4 | async-start | bytes 1310720 | tf_op jit(solution)/shard_map/all_to_all | solution.py:231
  65.6 0.7 reshape.38.weight_ref
  66.2 0.7 reshape.37.weight_ref
  66.9 0.7 reshape.36.weight_ref
  67.6 0.7 reshape.35.weight_ref
  68.9 0.9 pad_maximum_fusion.3.left_ref
  69.8 0.9 pad_maximum_fusion.left_ref
  70.6 0.9 pad_maximum_fusion.1.left_ref
  71.5 0.9 pad_maximum_fusion.2.left_ref
  72.4 8.8 %all-to-all-done.4.arrived_ref = bf16[32,80,128]{2,1,0:T(8,128)(2,1)S(1)} async-done(((bf16[32,80,128]{2,1,0:T(8,128)(2,1)}), bf16[32,80,128]{2,1,0:T(8,128)(2,1)S(1)}, u32[]{:S(2)}, u32[]{:S(2)}) %all-to-all-start.4) | async-done | bytes 655392 | tf_op jit(solution)/shard_map/all_to_all | solution.py:231
  81.2 5.1 %all-to-all-start.1 = ((bf16[32,80,128]{2,1,0:T(8,128)(2,1)}), bf16[32,80,128]{2,1,0:T(8,128)(2,1)S(1)}, u32[]{:S(2)}, u32[]{:S(2)}) async-start(bf16[32,80,128]{2,1,0:T(8,128)(2,1)} %get-tuple-element.11), calls=%async_computation.1 | async-start | bytes 1310720 | tf_op jit(solution)/shard_map/all_to_all | solution.py:233
  86.9 0.6 broadcast_bitcast_fusion.3.edge_ref
  87.6 0.6 broadcast_bitcast_fusion.2.edge_ref
  89.3 0.7 reduce.3
  90.6 5.7 %add_chunk.4.rest_0_ = f32[22,128,128]{2,1,0:T(8,128)} custom-call(s32[32]{0:T(128)} %reshape.34.meta_ref, bf16[32,80,128]{2,1,0:T(8,128)(2,1)} %copy-done.1, bf16[4,128,240]{2,1,0:T(8,128)(2,1)} %pad_maximum_fusion.3.left_ref, f32[9,240]{1,0:T(8,128)} %reshape.38.weight_ref, f32[80,128]{1,0:T(8,128)} %broadcast_bitcast_fusion.edge_ref), custom_call_target="tpu_custom_call" | custom-call | flops 849346560 | bytes 3538944 | tf_op jit(solution)/shard_map/add_chunk/pallas_call | solution.py:174
  96.3 6.3 %add_chunk.5.rest_0_ = f32[22,128,128]{2,1,0:T(8,128)} custom-call(s32[32]{0:T(128)} %reshape.34.meta_ref, bf16[32,80,128]{2,1,0:T(8,128)(2,1)} %copy-done, bf16[4,128,240]{2,1,0:T(8,128)(2,1)} %pad_maximum_fusion.2.left_ref, f32[9,240]{1,0:T(8,128)} %reshape.37.weight_ref, f32[80,128]{1,0:T(8,128)} %broadcast_bitcast_fusion.1.edge_ref, ...), custom_call_target="tpu_custom_call" | custom-call | flops 849346560 | bytes 3538944 | tf_op jit(solution)/shard_map/add_chunk/pallas_call | solution.py:174
  102.6 6.3 %add_chunk.6.rest_0_ = f32[22,128,128]{2,1,0:T(8,128)} custom-call(s32[32]{0:T(128)} %reshape.34.meta_ref, bf16[32,80,128]{2,1,0:T(8,128)(2,1)} %all_to_all.30.arrived_ref, bf16[4,128,240]{2,1,0:T(8,128)(2,1)} %pad_maximum_fusion.1.left_ref, f32[9,240]{1,0:T(8,128)} %reshape.36.weight_ref, f32[80,128]{1,0:T(8,128)} %broadcast_bitcast_fusion.2.edge_ref, ...), custom_call_target="tpu_custom_call" | custom-call | flops 849346560 | bytes 3538944 | tf_op jit(solution)/shard_map/add_chunk/pallas_call | solution.py:174
  108.9 0.9 copy-done.2
  109.7 6.6 %add_chunk.7.scores_ref = f32[6,128,128]{2,1,0:T(8,128)} custom-call(s32[32]{0:T(128)} %reshape.34.meta_ref, bf16[32,80,128]{2,1,0:T(8,128)(2,1)} %copy-done.2, bf16[4,128,240]{2,1,0:T(8,128)(2,1)} %pad_maximum_fusion.left_ref, f32[9,240]{1,0:T(8,128)} %reshape.35.weight_ref, f32[80,128]{1,0:T(8,128)} %broadcast_bitcast_fusion.3.edge_ref, ...), custom_call_target="tpu_custom_call" | custom-call | flops 849346560 | bytes 3538944 | tf_op jit(solution)/shard_map/add_chunk/pallas_call | solution.py:174
  116.3 0.9 fusion.3
  117.2 9.3 %collective-permute-start.1 = (f32[1,128,128]{2,1,0:T(8,128)S(1)}, f32[1,128,128]{2,1,0:T(8,128)S(1)}, u32[]{:S(2)}, u32[]{:S(2)}) collective-permute-start(f32[1,128,128]{2,1,0:T(8,128)S(1)} %get-tuple-element.15), channel_id=1, source_target_pairs={{1,0},{2,1},{3,2},{4,3},{5,4},{6,5},{7,6},{8,7},{9,8},{10,9},{11,1... | collective-permute-start | bytes 196616 | tf_op jit(solution)/shard_map/ppermute | solution.py:249
  126.5 1.9 %collective-permute-start = (f32[1,128,128]{2,1,0:T(8,128)S(1)}, f32[1,128,128]{2,1,0:T(8,128)S(1)}, u32[]{:S(2)}, u32[]{:S(2)}) collective-permute-start(f32[1,128,128]{2,1,0:T(8,128)S(1)} %get-tuple-element.16), channel_id=1, source_target_pairs={{0,1},{1,2},{2,3},{3,4},{4,5},{5,6},{6,7},{7,8},{8,9},{9,10},{10,1... | collective-permute-start | bytes 196616 | tf_op jit(solution)/shard_map/ppermute | solution.py:248
  128.5 4.5 %collective-permute-done.before_ref = f32[1,128,128]{2,1,0:T(8,128)S(1)} collective-permute-done((f32[1,128,128]{2,1,0:T(8,128)S(1)}, f32[1,128,128]{2,1,0:T(8,128)S(1)}, u32[]{:S(2)}, u32[]{:S(2)}) %collective-permute-start) | collective-permute-done | bytes 65568 | tf_op jit(solution)/shard_map/ppermute | solution.py:248
  133.0 0.6 copy-done.5
  133.6 1.8 %depth_rows.1 = f32[4,128]{1,0:T(4,128)} custom-call(f32[6,128,128]{2,1,0:T(8,128)} %add_chunk.7.scores_ref, f32[1,128,128]{2,1,0:T(8,128)} %copy-done.5, f32[1,128,128]{2,1,0:T(8,128)} %copy-done.4), custom_call_target="tpu_custom_call" | custom-call | tf_op jit(solution)/shard_map/depth_rows/pallas_call | solution.py:212
  (30 shorter events, 3.9 us)
Async XLA Ops:
  4.3 39.4 %copy-start.6 = (f32[40,3,3,3]{0,3,2,1:T(4,128)S(1)}, f32[40,3,3,3]{0,3,2,1:T(4,128)}, u32[]{:S(2)}) copy-start(f32[40,3,3,3]{0,3,2,1:T(4,128)} %param.11) | copy-start | bytes 12964
  4.4 39.5 %copy-start.3 = (bf16[4,320,128]{2,1,0:T(8,128)(2,1)S(1)}, bf16[4,320,128]{2,1,0:T(8,128)(2,1)}, u32[]{:S(2)}) copy-start(bf16[4,320,128]{2,1,0:T(8,128)(2,1)} %param.10) | copy-start | bytes 983044
  39.1 20.9 %all-to-all-start.3 = ((bf16[32,80,128]{2,1,0:T(8,128)(2,1)}), bf16[32,80,128]{2,1,0:T(8,128)(2,1)S(1)}, u32[]{:S(2)}, u32[]{:S(2)}) async-start(bf16[32,80,128]{2,1,0:T(8,128)(2,1)} %get-tuple-element.13), calls=%async_computation.3 | async-start | bytes 1310720 | tf_op jit(solution)/shard_map/all_to_all | solution.py:233
  59.9 8.9 %copy-start = (bf16[32,80,128]{2,1,0:T(8,128)(2,1)}, bf16[32,80,128]{2,1,0:T(8,128)(2,1)S(1)}, u32[]{:S(2)}) copy-start(bf16[32,80,128]{2,1,0:T(8,128)(2,1)S(1)} %all-to-all-done.3.arrived_ref) | copy-start | bytes 1966084
  59.9 21.2 %all-to-all-start.4 = ((bf16[32,80,128]{2,1,0:T(8,128)(2,1)}), bf16[32,80,128]{2,1,0:T(8,128)(2,1)S(1)}, u32[]{:S(2)}, u32[]{:S(2)}) async-start(bf16[32,80,128]{2,1,0:T(8,128)(2,1)} %get-tuple-element.14), calls=%async_computation.4 | async-start | bytes 1310720 | tf_op jit(solution)/shard_map/all_to_all | solution.py:231
  81.2 9.4 %copy-start.1 = (bf16[32,80,128]{2,1,0:T(8,128)(2,1)}, bf16[32,80,128]{2,1,0:T(8,128)(2,1)S(1)}, u32[]{:S(2)}) copy-start(bf16[32,80,128]{2,1,0:T(8,128)(2,1)S(1)} %all-to-all-done.4.arrived_ref) | copy-start | bytes 1966084
  81.2 27.7 %all-to-all-start.1 = ((bf16[32,80,128]{2,1,0:T(8,128)(2,1)}), bf16[32,80,128]{2,1,0:T(8,128)(2,1)S(1)}, u32[]{:S(2)}, u32[]{:S(2)}) async-start(bf16[32,80,128]{2,1,0:T(8,128)(2,1)} %get-tuple-element.11), calls=%async_computation.1 | async-start | bytes 1310720 | tf_op jit(solution)/shard_map/all_to_all | solution.py:233
  108.8 0.9 copy-start.2
  117.2 11.2 %collective-permute-start.1 = (f32[1,128,128]{2,1,0:T(8,128)S(1)}, f32[1,128,128]{2,1,0:T(8,128)S(1)}, u32[]{:S(2)}, u32[]{:S(2)}) collective-permute-start(f32[1,128,128]{2,1,0:T(8,128)S(1)} %get-tuple-element.15), channel_id=1, source_target_pairs={{1,0},{2,1},{3,2},{4,3},{5,4},{6,5},{7,6},{8,7},{9,8},{10,9},{11,1... | collective-permute-start | bytes 196616 | tf_op jit(solution)/shard_map/ppermute | solution.py:249
  126.5 6.5 %collective-permute-start = (f32[1,128,128]{2,1,0:T(8,128)S(1)}, f32[1,128,128]{2,1,0:T(8,128)S(1)}, u32[]{:S(2)}, u32[]{:S(2)}) collective-permute-start(f32[1,128,128]{2,1,0:T(8,128)S(1)} %get-tuple-element.16), channel_id=1, source_target_pairs={{0,1},{1,2},{2,3},{3,4},{4,5},{5,6},{6,7},{7,8},{8,9},{9,10},{10,1... | collective-permute-start | bytes 196616 | tf_op jit(solution)/shard_map/ppermute | solution.py:248
  128.4 4.5 %copy-start.4 = (f32[1,128,128]{2,1,0:T(8,128)}, f32[1,128,128]{2,1,0:T(8,128)S(1)}, u32[]{:S(2)}) copy-start(f32[1,128,128]{2,1,0:T(8,128)S(1)} %collective-permute-done.1.after_ref) | copy-start | bytes 196612
  133.0 0.6 copy-start.5

commit v2 on v0

v2 whole, which is shorter than its diff:
```python
import functools

import jax
import jax.numpy as jnp
from jax import lax
from jax.experimental import pallas as pl
from jax.experimental.pallas import tpu as pltpu
from jax.sharding import PartitionSpec as P

CG = 8
DISP = 96
DSPAN = 16
CAP = 2
SETS = 2

VMEM = pl.BlockSpec(memory_space=pltpu.VMEM)
SMEM = pl.BlockSpec(memory_space=pltpu.SMEM)
ANY = pl.BlockSpec(memory_space=pl.ANY)


def pack_kernel(half, span, code_ref, source_ref, out_ref, count_ref, sem):
    items = source_ref.shape[0]

    @pl.loop(0, half * SETS)
    def _(s):
        count_ref[s] = 0

    @pl.loop(0, items)
    def _(i):
        owner = lax.div(code_ref[i], span)
        place = lax.rem(owner, half) * SETS + lax.div(owner, half)
        slot = place * CAP + count_ref[place]
        count_ref[place] = count_ref[place] + 1
        pltpu.make_async_copy(source_ref.at[i], out_ref.at[slot], sem).start()

    @pl.loop(0, items)
    def _(i):
        pltpu.make_async_copy(source_ref.at[0], out_ref.at[0], sem).wait()


def pack_rows(codes, source, half, span):
    items, channels, pixels = source.shape
    slots = half * SETS * CAP
    return pl.pallas_call(
        functools.partial(pack_kernel, half, span),
        out_shape=jax.ShapeDtypeStruct((slots, channels, pixels), source.dtype),
        in_specs=[SMEM, VMEM],
        out_specs=ANY,
        scratch_shapes=[pltpu.SMEM((half * SETS,), jnp.int32), pltpu.SemaphoreType.DMA],
        name="pack_rows",
    )(codes, source)


def table_kernel(half, rows, code_ref, table_ref, state_ref):
    views, items = code_ref.shape
    span = rows * DSPAN
    room = half * CAP
    me = lax.axis_index("views")
    owners = (me, lax.rem(me + half, views))

    @pl.loop(0, SETS + SETS * rows)
    def _(j):
        table_ref[SETS * room + j] = 0

    @pl.loop(0, views)
    def _(p):
        home = lax.rem(me ^ p, half)
        for t in range(SETS):
            state_ref[t] = 0

        @pl.loop(0, items)
        def _(i):
            owner = lax.div(code_ref[p, i], span)
            rest = lax.rem(code_ref[p, i], span)
            for t in range(SETS):

                @pl.when(owner == owners[t])
                def _():
                    count = SETS * room + SETS + t * rows + lax.div(rest, DSPAN)
                    table_ref[count] = table_ref[count] + 1

                    @pl.when(p < half)
                    def _():
                        place = home * SETS + lax.div(owners[t], half)
                        entry = table_ref[SETS * room + t]
                        slot = place * CAP + state_ref[t]
                        table_ref[t * room + entry] = slot * span + rest
                        table_ref[SETS * room + t] = entry + 1
                        state_ref[t] = state_ref[t] + 1


def make_table(codes, half, rows):
    length = SETS * (half * CAP + 1 + rows)
    return pl.pallas_call(
        functools.partial(table_kernel, half, rows),
        out_shape=jax.ShapeDtypeStruct((length,), jnp.int32),
        in_specs=[SMEM],
        out_specs=SMEM,
        scratch_shapes=[pltpu.SMEM((SETS,), jnp.int32)],
        name="make_table",
    )(codes)


def split_two(values):
    high = values.astype(jnp.bfloat16)
    return high, (values - high.astype(jnp.float32)).astype(jnp.bfloat16)


def both_parts(values):
    return jnp.concatenate(split_two(values), axis=1)


def shift_left(values, offset):
    lane = lax.broadcasted_iota(jnp.int32, values.shape, 1)
    pixels = values.shape[1]
    moved = pltpu.roll(values, (-offset) % pixels, 1)
    return jnp.where((lane + offset >= 0) & (lane + offset < pixels), moved, 0.0)


def spread(values):
    groups, pixels = values.shape
    wide = jnp.broadcast_to(values[:, None, :], (groups, CG, pixels))
    return wide.reshape(groups * CG, pixels)


def set_kernel(
    t, room, table_ref, arrived_ref, left_ref, weight_ref, edge_ref,
    main_ref, low_ref, high_ref, stack_ref, wide_ref, total_ref, canvas_ref,
):
    slots, channels, pixels = arrived_ref.shape
    rows = left_ref.shape[0]
    span = rows * DSPAN
    lane = lax.broadcasted_iota(jnp.int32, (channels, pixels), 1)
    total_ref[...] = jnp.zeros_like(total_ref)
    canvas_ref[...] = jnp.zeros_like(canvas_ref)

    def add_slot(entry, carry):
        code = table_ref[t * room + entry]
        slot = lax.div(code, span)
        row = lax.div(lax.rem(code, span), DSPAN)
        begin = lax.rem(code, DSPAN)
        moved = pltpu.roll(arrived_ref[slot].astype(jnp.float32), begin, 1)
        canvas_ref[row] = canvas_ref[row] + jnp.where(lane >= begin, moved, 0.0)
        return carry

    lax.fori_loop(0, table_ref[SETS * room + t], add_slot, 0)

    @pl.loop(0, rows)
    def _(r):
        count = table_ref[SETS * room + SETS + t * rows + r]
        divisor = jnp.full((channels, pixels), jnp.maximum(count, 1).astype(jnp.float32))
        mean = canvas_ref[r] / divisor
        for e in range(3):
            stack_ref[r, e * channels : (e + 1) * channels, :] = shift_left(mean, e - 1)
        edge = jnp.broadcast_to(mean[:, :1], (channels, pixels)) * spread(edge_ref[...])
        wide = jnp.dot(
            left_ref[r, :, 2 * channels :],
            both_parts(edge),
            preferred_element_type=jnp.float32,
        )
        total_ref[(rows + 2) * 3 + r] = wide[:, :pixels] + wide[:, pixels:]

    @pl.loop(0, 9)
    def _(tap):
        wide_ref[...] = spread(weight_ref[tap])
        for r in range(rows):
            right = both_parts(stack_ref[r] * wide_ref[...])
            wide = jnp.dot(left_ref[r], right, preferred_element_type=jnp.float32)
            place = (r + 2 - lax.div(tap, 3)) * 3 + lax.rem(tap, 3)
            total_ref[place] = total_ref[place] + (wide[:, :pixels] + wide[:, pixels:])

    x = lax.broadcasted_iota(jnp.int32, (pixels, pixels), 0)
    v = lax.broadcasted_iota(jnp.int32, (pixels, pixels), 1)
    inside = (x >= v) & (x - v < DISP)
    border = (x < DISP - 1) & ((v >= pixels - 2) | (v < 1))
    for r in range(rows + 2):
        total = jnp.where(inside, total_ref[3 * r + 1], 0.0)
        for b in (0, 2):
            kept = jnp.where(inside, total_ref[3 * r + b], 0.0)
            total = total + pltpu.roll(kept, (b - 1) % pixels, 1)
        for a in range(3):
            if 0 <= r + a - 2 < rows:
                edge = total_ref[(rows + 2) * 3 + r + a - 2]
                moved = pltpu.roll(edge, (-8 * a) % pixels, 1) if a else edge
                total = total + jnp.where(border, moved, 0.0)
        step = 1
        while step < pixels:
            moved = pltpu.roll(total, pixels - step, 1)
            total = jnp.where(((x + 1) & step) != 0, moved, total)
            step *= 2
        kept = total.T[pixels - DISP :]
        if r == 0:
            low_ref[0] = kept
        elif r == rows + 1:
            high_ref[0] = kept
        else:
            main_ref[r - 1] = kept


def add_set(t, table, arrived, left, weight, edge):
    slots, channels, pixels = arrived.shape
    rows = left.shape[0]
    room = slots // SETS
    shapes = [(n, DISP, pixels) for n in (rows, 1, 1)]
    return pl.pallas_call(
        functools.partial(set_kernel, t, room),
        out_shape=[jax.ShapeDtypeStruct(shape, jnp.float32) for shape in shapes],
        in_specs=[SMEM] + [VMEM] * 4,
        out_specs=[VMEM] * 3,
        scratch_shapes=[
            pltpu.VMEM((rows, 3 * channels, pixels), jnp.float32),
            pltpu.VMEM((3 * channels, pixels), jnp.float32),
            pltpu.VMEM(((rows + 2) * 3 + rows, pixels, pixels), jnp.float32),
            pltpu.VMEM((rows, channels, pixels), jnp.float32),
        ],
        cost_estimate=pl.CostEstimate(
            flops=2 * rows * 9 * pixels * 2 * pixels * 3 * channels,
            bytes_accessed=2 * slots * channels * pixels,
            transcendentals=0,
        ),
        name="add_set",
    )(table, arrived, left, weight, edge)


def depth_kernel(own_ref, far_ref, before_ref, before_far_ref, after_ref, after_far_ref, out_ref):
    rows, pixels = out_ref.shape
    level = (DISP - 1) - lax.broadcasted_iota(jnp.int32, (DISP, pixels), 0)
    share = level.astype(jnp.float32) / DISP
    for r in range(rows):
        scores = own_ref[r] + far_ref[r]
        if r == 0:
            scores = scores + (before_ref[0] + before_far_ref[0])
        if r == rows - 1:
            scores = scores + (after_ref[0] + after_far_ref[0])
        weights = jnp.exp(scores - jnp.max(scores, axis=0, keepdims=True))
        bottom = jnp.sum(weights, axis=0, keepdims=True)
        out_ref[r : r + 1, :] = jnp.sum(weights * share, axis=0, keepdims=True) / bottom


def depth_rows(*parts):
    rows, _, pixels = parts[0].shape
    return pl.pallas_call(
        depth_kernel,
        out_shape=jax.ShapeDtypeStruct((rows, pixels), jnp.float32),
        in_specs=[VMEM] * len(parts),
        out_specs=VMEM,
        name="depth_rows",
    )(*parts)


def stack_left(reference_rows):
    pixels = reference_rows.shape[2]
    padded = jnp.pad(jnp.swapaxes(reference_rows, 1, 2), ((0, 0), (1, 1), (0, 0)))
    return jnp.concatenate([padded[:, e : e + pixels] for e in range(3)], axis=2)


def gather_codes(codes, views):
    gathered = codes[None]
    step = 1
    while step < views:
        other = lax.ppermute(gathered, "views", [(i, i ^ step) for i in range(views)])
        gathered = jnp.concatenate([gathered, other], axis=0)
        step *= 2
    return gathered


def body(source_rows, route_owner, target_row, start_index, reference_rows, conv_weight):
    views = lax.axis_size("views")
    half = views // 2
    rows, channels, pixels = reference_rows.shape
    span = rows * DSPAN
    send = functools.partial(lax.ppermute, axis_name="views")
    far_rows = send(reference_rows, perm=[(i, (i + half) % views) for i in range(views)])
    codes = route_owner[:, 0] * span + target_row * DSPAN + start_index
    packed = pack_rows(codes, source_rows, half, span)
    arrived = lax.all_to_all(
        packed,
        "views",
        split_axis=0,
        concat_axis=0,
        tiled=True,
        axis_index_groups=[list(range(half)), list(range(half, views))],
    )
    table = make_table(gather_codes(codes, views), half, rows)

    scaled = conv_weight / CG
    taps = scaled.transpose(1, 2, 3, 0).reshape(9, -1, 1)
    taps = jnp.broadcast_to(taps, taps.shape[:2] + (pixels,))
    edges = jnp.pad(scaled[..., 2], ((0, 0), (0, 0), (0, 5))).reshape(-1, 24)
    edges = jnp.roll(jnp.pad(edges, ((0, 0), (0, pixels - 24))), -2, 1)
    near, far = stack_left(reference_rows), stack_left(far_rows)

    far_main, far_low, far_high = add_set(1, table, arrived, far, taps, edges)
    home = [(i, (i + half) % views) for i in range(views)]
    other_main = send(far_main, perm=home)
    other_low = send(far_low, perm=[(i, j - 1) for i, j in home if j > 0])
    other_high = send(far_high, perm=[(i, j + 1) for i, j in home if j + 1 < views])
    own_main, own_low, own_high = add_set(0, table, arrived, near, taps, edges)
    own_low = send(own_low, perm=[(i, i - 1) for i in range(1, views)])
    own_high = send(own_high, perm=[(i, i + 1) for i in range(views - 1)])
    return depth_rows(own_main, other_main, own_high, other_high, own_low, other_low)


def solution(mesh):
    in_specs = (
        P(("groups", "views"), None, None),
        P(("groups", "views"), None),
        P(("groups", "views")),
        P(("groups", "views")),
        P(("groups", "views"), None, None),
        P(),
    )
    out_specs = P(("groups", "views"), None)
    return jax.shard_map(body, mesh=mesh, in_specs=in_specs, out_specs=out_specs, check_vma=False)
```

time: 213 us -> 110 us (0.52)
  the two profiles are of different devices: /device:TPU:17 before, /device:TPU:1 now
where the time goes in v2:
time: 110 us
  Pallas kernels  37.1 us (34%)
  waiting for transfers between devices  33.9 us (31%)
  starting transfers between devices  30.1 us (27%)
  other arithmetic  4.47 us (4%)
  local copies, waits for them, and re-layouts  4.35 us (4%)
    ppermute x4, waiting for transfers between devices, gather_codes(): lax.ppermute(gathered, 'views', [(i, i ^ step) for i in range(views)])  29.7 us
    pallas_call x2, Pallas kernels, add_set(): pl.pallas_call(functools.partial(set_kernel, t, room), out_shape=[jax.Sha...  25.6 us
    ppermute x4, starting transfers between devices, gather_codes(): lax.ppermute(gathered, 'views', [(i, i ^ step) for i in range(views)])  7.48 us
    pallas_call x1, Pallas kernels, make_table(): pl.pallas_call(functools.partial(table_kernel, half, rows), out_shape=jax...  7.45 us
    all_to_all x1, starting transfers between devices, body(): lax.all_to_all(packed, 'views', split_axis=0, concat_axis=0, tiled=True,...  5.46 us
    ppermute x1, waiting for transfers between devices, body(): other_low = send(far_low, perm=[(i, j - 1) for i, j in home if j > 0])  4.15 us
    ppermute x1, starting transfers between devices, body(): other_low = send(far_low, perm=[(i, j - 1) for i, j in home if j > 0])  4.08 us
    ppermute x1, starting transfers between devices, body(): own_high = send(own_high, perm=[(i, i + 1) for i in range(views - 1)])  3.45 us
  transfers between devices with their start and end apart: 11, of which 4 were waited for; matrix products, arithmetic and copies ran while one was open for 5% of the time, Pallas kernels for 19%

profile of v2, /device:TPU:1, one launch (start us, length us, event | category | flops | bytes accessed | tf_op | source)
XLA Modules:
  0.0 110.1 jit_solution(16312556505460827524)
XLA Ops:
  0.0 1.2 %fusion.code_ref = s32[12]{0:T(128)} fusion(s32[12]{0:T(128)} %param.9, s32[12]{0:T(128)} %param.8, s32[12,1]{0,1:T(1,128)} %param.7), kind=kLoop, calls=%fused_computation.15 | loop fusion | flops 48 | bytes 192 | tf_op jit(solution)/shard_map/add | solution.py:274
  1.2 2.3 %pack_rows.1 = bf16[32,320,128]{2,1,0:T(8,128)(2,1)} custom-call(s32[12]{0:T(128)} %fusion.code_ref, bf16[12,320,128]{2,1,0:T(8,128)(2,1)} %source_ref.1), custom_call_target="tpu_custom_call" | custom-call | tf_op jit(solution)/shard_map/pack_rows/pallas_call | solution.py:44
  3.5 5.5 %all-to-all-start = ((bf16[32,320,128]{2,1,0:T(8,128)(2,1)}), bf16[32,320,128]{2,1,0:T(8,128)(2,1)S(1)}, u32[]{:S(2)}, u32[]{:S(2)}) async-start(bf16[32,320,128]{2,1,0:T(8,128)(2,1)} %pack_rows.1), calls=%async_computation | async-start | bytes 5242880 | tf_op jit(solution)/shard_map/all_to_all | solution.py:276
  9.1 0.2 copy.10
  9.3 2.4 %collective-permute-start.4 = (bf16[4,320,128]{1,2,0:T(8,128)(2,1)S(1)}, bf16[4,320,128]{1,2,0:T(8,128)(2,1)S(1)}, u32[]{:S(2)}, u32[]{:S(2)}) collective-permute-start(bf16[4,320,128]{1,2,0:T(8,128)(2,1)S(1)} %copy.10), channel_id=1, source_target_pairs={{0,8},{1,9},{2,10},{3,11},{4,12},{5,13},{6,14},{7,15},{8,0},{9,1},... | collective-permute-start | bytes 983048 | tf_op jit(solution)/shard_map/ppermute | solution.py:273
  11.7 0.2 pad_slice_fusion.3
  11.9 1.3 %pad_maximum_fusion.left_ref = bf16[4,128,960]{2,1,0:T(8,128)(2,1)} fusion(bf16[4,128,320]{2,1,0:T(8,128)(2,1)S(1)} %get-tuple-element.20, bf16[4,128,320]{2,1,0:T(8,128)(2,1)S(1)} %bitcast.16, bf16[4,128,320]{2,1,0:T(8,128)(2,1)S(1)} %get-tuple-element.19), kind=kLoop, calls=%fused_computation | loop fusion | flops 2949120 | bytes 1966080 | tf_op jit(solution)/shard_map/concatenate | solution.py:254
  13.2 1.7 %collective-permute-start.1 = (s32[2,12]{1,0:T(2,128)S(1)}, s32[2,12]{1,0:T(2,128)S(1)}, u32[]{:S(2)}, u32[]{:S(2)}) collective-permute-start(s32[2,12]{1,0:T(2,128)S(1)} %pad_add_fusion.2), channel_id=1, source_target_pairs={{0,2},{1,3},{2,0},{3,1},{4,6},{5,7},{6,4},{7,5},{8,10},{9,11},{10,... | collective-permute-start | bytes 296 | tf_op jit(solution)/shard_map/ppermute | solution.py:261
  15.0 22.0 %collective-permute-done.1 = s32[2,12]{1,0:T(2,128)S(1)} collective-permute-done((s32[2,12]{1,0:T(2,128)S(1)}, s32[2,12]{1,0:T(2,128)S(1)}, u32[]{:S(2)}, u32[]{:S(2)}) %collective-permute-start.1) | collective-permute-done | bytes 128 | tf_op jit(solution)/shard_map/ppermute | solution.py:261
  37.0 3.6 %collective-permute-start.2 = (s32[4,12]{1,0:T(4,128)S(1)}, s32[4,12]{1,0:T(4,128)S(1)}, u32[]{:S(2)}, u32[]{:S(2)}) collective-permute-start(s32[4,12]{1,0:T(4,128)S(1)} %pad_add_fusion.1), channel_id=1, source_target_pairs={{0,4},{1,5},{2,6},{3,7},{4,0},{5,1},{6,2},{7,3},{8,12},{9,13},{10,... | collective-permute-start | bytes 584 | tf_op jit(solution)/shard_map/ppermute | solution.py:261
  40.6 7.2 %collective-permute-done.2 = s32[4,12]{1,0:T(4,128)S(1)} collective-permute-done((s32[4,12]{1,0:T(4,128)S(1)}, s32[4,12]{1,0:T(4,128)S(1)}, u32[]{:S(2)}, u32[]{:S(2)}) %collective-permute-start.2) | collective-permute-done | bytes 224 | tf_op jit(solution)/shard_map/ppermute | solution.py:261
  47.8 2.1 %collective-permute-start.3 = (s32[8,12]{1,0:T(8,128)S(1)}, s32[8,12]{1,0:T(8,128)S(1)}, u32[]{:S(2)}, u32[]{:S(2)}) collective-permute-start(s32[8,12]{1,0:T(8,128)S(1)} %pad_add_fusion), channel_id=1, source_target_pairs={{0,8},{1,9},{2,10},{3,11},{4,12},{5,13},{6,14},{7,15},{8,0},{9,1},... | collective-permute-start | bytes 1160 | tf_op jit(solution)/shard_map/ppermute | solution.py:261
  49.9 0.7 pad_maximum_fusion.2.edge_ref
  50.6 0.1 broadcast_in_dim.11
  50.7 0.6 collective-permute-done.3
  51.2 1.2 %concatenate.28.code_ref = s32[16,12]{1,0:T(8,128)} concatenate(s32[1,12]{1,0:T(1,128)S(1)} %bitcast.25, s32[1,12]{1,0:T(1,128)S(1)} %collective-permute-done, s32[2,12]{1,0:T(2,128)S(1)} %collective-permute-done.1, s32[4,12]{1,0:T(4,128)S(1)} %collective-permute-done.2, s32[8,12]{1,0:T(8,128)S(1)} %collective-permute-done.3), dimensions={0} | concatenate | bytes 1536 | tf_op jit(solution)/shard_map/concatenate | solution.py:262
  52.4 7.5 %make_table.1.table_ref = s32[42]{0:T(128)} custom-call(s32[16,12]{1,0:T(8,128)} %concatenate.28.code_ref), custom_call_target="tpu_custom_call" | custom-call | tf_op jit(solution)/shard_map/make_table/pallas_call | solution.py:94
  59.9 0.2 pad_slice_fusion.1
  60.1 1.3 %pad_maximum_fusion.1.left_ref = bf16[4,128,960]{2,1,0:T(8,128)(2,1)} fusion(bf16[4,128,320]{2,1,0:T(8,128)(2,1)S(1)} %get-tuple-element.18, bf16[4,128,320]{2,1,0:T(8,128)(2,1)S(1)} %bitcast.18, bf16[4,128,320]{2,1,0:T(8,128)(2,1)S(1)} %get-tuple-element.17), kind=kLoop, calls=%fused_computation.1 | loop fusion | flops 2949120 | bytes 1966080 | tf_op jit(solution)/shard_map/concatenate | solution.py:254
  61.4 1.2 %broadcast_in_dim.12.weight_ref = f32[9,120,128]{2,1,0:T(8,128)} broadcast(f32[9,120]{1,0:T(8,128)S(1)} %broadcast_in_dim.11), dimensions={0,1} | broadcast | bytes 557280 | tf_op jit(solution)/shard_map/broadcast_in_dim | solution.py:288
  62.5 0.5 copy-done
  63.0 12.4 %add_set.3 = (f32[4,96,128]{2,1,0:T(8,128)}, f32[1,96,128]{2,1,0:T(8,128)}, f32[1,96,128]{2,1,0:T(8,128)}) custom-call(s32[42]{0:T(128)} %make_table.1.table_ref, bf16[32,320,128]{2,1,0:T(8,128)(2,1)} %copy-done, bf16[4,128,960]{2,1,0:T(8,128)(2,1)} %pad_maximum_fusion.1.left_ref, f32[9,120,128]{2,1,0:T(8,128)} %broadcast_in_dim.12.weight_ref, ...), custom_call_target="tpu_custom_call" | custom-call | flops 2264924160 | bytes 2621440 | tf_op jit(solution)/shard_map/add_set/pallas_call | solution.py:205
  75.4 2.9 %collective-permute-start.5 = (f32[4,96,128]{2,1,0:T(8,128)}, f32[4,96,128]{2,1,0:T(8,128)S(1)}, u32[]{:S(2)}, u32[]{:S(2)}) collective-permute-start(f32[4,96,128]{2,1,0:T(8,128)} %get-tuple-element.12), channel_id=1, source_target_pairs={{0,8},{1,9},{2,10},{3,11},{4,12},{5,13},{6,14},{7,15},{8,0},{9,1},... | collective-permute-start | bytes 589832 | tf_op jit(solution)/shard_map/ppermute | solution.py:295
  78.3 13.2 %add_set.2 = (f32[4,96,128]{2,1,0:T(8,128)}, f32[1,96,128]{2,1,0:T(8,128)}, f32[1,96,128]{2,1,0:T(8,128)}) custom-call(s32[42]{0:T(128)} %make_table.1.table_ref, bf16[32,320,128]{2,1,0:T(8,128)(2,1)} %copy-done, bf16[4,128,960]{2,1,0:T(8,128)(2,1)} %pad_maximum_fusion.left_ref, f32[9,120,128]{2,1,0:T(8,128)} %broadcast_in_dim.12.weight_ref, ...), custom_call_target="tpu_custom_call" | custom-call | flops 2264924160 | bytes 2621440 | tf_op jit(solution)/shard_map/add_set/pallas_call | solution.py:205
  91.6 3.4 %collective-permute-start.6 = (f32[1,96,128]{2,1,0:T(8,128)}, f32[1,96,128]{2,1,0:T(8,128)S(1)}, u32[]{:S(2)}, u32[]{:S(2)}) collective-permute-start(f32[1,96,128]{2,1,0:T(8,128)} %get-tuple-element.13), channel_id=1, source_target_pairs={{0,1},{1,2},{2,3},{3,4},{4,5},{5,6},{6,7},{7,8},{8,9},{9,10},{10,1... | collective-permute-start | bytes 147464 | tf_op jit(solution)/shard_map/ppermute | solution.py:300
  95.0 1.9 %collective-permute-start.7 = (f32[1,96,128]{2,1,0:T(8,128)S(1)}, f32[1,96,128]{2,1,0:T(8,128)S(1)}, u32[]{:S(2)}, u32[]{:S(2)}) collective-permute-start(f32[1,96,128]{2,1,0:T(8,128)S(1)} %copy-done.10), channel_id=1, source_target_pairs={{0,9},{1,10},{2,11},{3,12},{4,13},{5,14},{6,15},{8,1},{9,2},{10,3}... | collective-permute-start | bytes 147464 | tf_op jit(solution)/shard_map/ppermute | solution.py:297
  97.0 2.4 %collective-permute-start.8 = (f32[1,96,128]{2,1,0:T(8,128)}, f32[1,96,128]{2,1,0:T(8,128)S(1)}, u32[]{:S(2)}, u32[]{:S(2)}) collective-permute-start(f32[1,96,128]{2,1,0:T(8,128)} %get-tuple-element.15), channel_id=1, source_target_pairs={{1,0},{2,1},{3,2},{4,3},{5,4},{6,5},{7,6},{8,7},{9,8},{10,9},{11,1... | collective-permute-start | bytes 147464 | tf_op jit(solution)/shard_map/ppermute | solution.py:299
  99.4 4.1 %collective-permute-start.9 = (f32[1,96,128]{2,1,0:T(8,128)S(1)}, f32[1,96,128]{2,1,0:T(8,128)S(1)}, u32[]{:S(2)}, u32[]{:S(2)}) collective-permute-start(f32[1,96,128]{2,1,0:T(8,128)S(1)} %copy-done.9), channel_id=1, source_target_pairs={{0,7},{1,8},{2,9},{3,10},{4,11},{5,12},{6,13},{7,14},{9,0},{10,1},... | collective-permute-start | bytes 147464 | tf_op jit(solution)/shard_map/ppermute | solution.py:296
  103.5 4.1 %collective-permute-done.9.after_far_ref = f32[1,96,128]{2,1,0:T(8,128)S(1)} collective-permute-done((f32[1,96,128]{2,1,0:T(8,128)S(1)}, f32[1,96,128]{2,1,0:T(8,128)S(1)}, u32[]{:S(2)}, u32[]{:S(2)}) %collective-permute-start.9) | collective-permute-done | bytes 49184 | tf_op jit(solution)/shard_map/ppermute | solution.py:296
  107.7 0.6 copy-done.6
  108.3 0.1 copy-done.2
  108.3 1.7 %depth_rows.1 = f32[4,128]{1,0:T(4,128)} custom-call(f32[4,96,128]{2,1,0:T(8,128)} %get-tuple-element.11.own_ref, f32[4,96,128]{2,1,0:T(8,128)} %copy-done.2, f32[1,96,128]{2,1,0:T(8,128)} %copy-done.3, f32[1,96,128]{2,1,0:T(8,128)} %copy-done.4, f32[1,96,128]{2,1,0:T(8,128)} %copy-done.5, f32[1,96,128]{2,1,0:T(8,128)} %copy-done.6), custom_call_target="tpu_custom_call" | custom-call | tf_op jit(solution)/shard_map/depth_rows/pallas_call | solution.py:242
  (36 shorter events, 0.3 us)
Async XLA Ops:
  3.5 5.5 %copy-start.8 = (s32[12]{0:T(128)S(1)}, s32[12]{0:T(128)}, u32[]{:S(2)}) copy-start(s32[12]{0:T(128)} %fusion.code_ref) | copy-start | bytes 148
  3.5 5.6 %copy-start.1 = (bf16[4,320,128]{2,1,0:T(8,128)(2,1)S(1)}, bf16[4,320,128]{2,1,0:T(8,128)(2,1)}, u32[]{:S(2)}) copy-start(bf16[4,320,128]{2,1,0:T(8,128)(2,1)} %param.10) | copy-start | bytes 983044
  3.5 8.2 %copy-start.7 = (f32[40,3,3,3]{0,3,2,1:T(4,128)S(1)}, f32[40,3,3,3]{0,3,2,1:T(4,128)}, u32[]{:S(2)}) copy-start(f32[40,3,3,3]{0,3,2,1:T(4,128)} %param.11) | copy-start | bytes 12964
  3.5 57.9 %all-to-all-start = ((bf16[32,320,128]{2,1,0:T(8,128)(2,1)}), bf16[32,320,128]{2,1,0:T(8,128)(2,1)S(1)}, u32[]{:S(2)}, u32[]{:S(2)}) async-start(bf16[32,320,128]{2,1,0:T(8,128)(2,1)} %pack_rows.1), calls=%async_computation | async-start | bytes 5242880 | tf_op jit(solution)/shard_map/all_to_all | solution.py:276
  9.0 4.2 %collective-permute-start = (s32[1,12]{1,0:T(1,128)S(1)}, s32[1,12]{1,0:T(1,128)S(1)}, u32[]{:S(2)}, u32[]{:S(2)}) collective-permute-start(s32[1,12]{1,0:T(1,128)S(1)} %bitcast.21), channel_id=1, source_target_pairs={{0,1},{1,0},{2,3},{3,2},{4,5},{5,4},{6,7},{7,6},{8,9},{9,8},{10,11... | collective-permute-start | bytes 152 | tf_op jit(solution)/shard_map/ppermute | solution.py:261
  9.3 50.6 %collective-permute-start.4 = (bf16[4,320,128]{1,2,0:T(8,128)(2,1)S(1)}, bf16[4,320,128]{1,2,0:T(8,128)(2,1)S(1)}, u32[]{:S(2)}, u32[]{:S(2)}) collective-permute-start(bf16[4,320,128]{1,2,0:T(8,128)(2,1)S(1)} %copy.10), channel_id=1, source_target_pairs={{0,8},{1,9},{2,10},{3,11},{4,12},{5,13},{6,14},{7,15},{8,0},{9,1},... | collective-permute-start | bytes 983048 | tf_op jit(solution)/shard_map/ppermute | solution.py:273
  13.2 23.8 %collective-permute-start.1 = (s32[2,12]{1,0:T(2,128)S(1)}, s32[2,12]{1,0:T(2,128)S(1)}, u32[]{:S(2)}, u32[]{:S(2)}) collective-permute-start(s32[2,12]{1,0:T(2,128)S(1)} %pad_add_fusion.2), channel_id=1, source_target_pairs={{0,2},{1,3},{2,0},{3,1},{4,6},{5,7},{6,4},{7,5},{8,10},{9,11},{10,... | collective-permute-start | bytes 296 | tf_op jit(solution)/shard_map/ppermute | solution.py:261
  37.0 10.8 %collective-permute-start.2 = (s32[4,12]{1,0:T(4,128)S(1)}, s32[4,12]{1,0:T(4,128)S(1)}, u32[]{:S(2)}, u32[]{:S(2)}) collective-permute-start(s32[4,12]{1,0:T(4,128)S(1)} %pad_add_fusion.1), channel_id=1, source_target_pairs={{0,4},{1,5},{2,6},{3,7},{4,0},{5,1},{6,2},{7,3},{8,12},{9,13},{10,... | collective-permute-start | bytes 584 | tf_op jit(solution)/shard_map/ppermute | solution.py:261
  47.8 3.4 %collective-permute-start.3 = (s32[8,12]{1,0:T(8,128)S(1)}, s32[8,12]{1,0:T(8,128)S(1)}, u32[]{:S(2)}, u32[]{:S(2)}) collective-permute-start(s32[8,12]{1,0:T(8,128)S(1)} %pad_add_fusion), channel_id=1, source_target_pairs={{0,8},{1,9},{2,10},{3,11},{4,12},{5,13},{6,14},{7,15},{8,0},{9,1},... | collective-permute-start | bytes 1160 | tf_op jit(solution)/shard_map/ppermute | solution.py:261
  61.4 1.6 %copy-start = (bf16[32,320,128]{2,1,0:T(8,128)(2,1)}, bf16[32,320,128]{2,1,0:T(8,128)(2,1)S(1)}, u32[]{:S(2)}) copy-start(bf16[32,320,128]{2,1,0:T(8,128)(2,1)S(1)} %all-to-all-done.arrived_ref) | copy-start | bytes 7864324
  75.4 19.6 %copy-start.10 = (f32[1,96,128]{2,1,0:T(8,128)S(1)}, f32[1,96,128]{2,1,0:T(8,128)}, u32[]{:S(2)}) copy-start(f32[1,96,128]{2,1,0:T(8,128)} %get-tuple-element.14) | copy-start | bytes 147460
  75.4 24.0 %copy-start.9 = (f32[1,96,128]{2,1,0:T(8,128)S(1)}, f32[1,96,128]{2,1,0:T(8,128)}, u32[]{:S(2)}) copy-start(f32[1,96,128]{2,1,0:T(8,128)} %get-tuple-element.16) | copy-start | bytes 147460
  75.4 32.3 %collective-permute-start.5 = (f32[4,96,128]{2,1,0:T(8,128)}, f32[4,96,128]{2,1,0:T(8,128)S(1)}, u32[]{:S(2)}, u32[]{:S(2)}) collective-permute-start(f32[4,96,128]{2,1,0:T(8,128)} %get-tuple-element.12), channel_id=1, source_target_pairs={{0,8},{1,9},{2,10},{3,11},{4,12},{5,13},{6,14},{7,15},{8,0},{9,1},... | collective-permute-start | bytes 589832 | tf_op jit(solution)/shard_map/ppermute | solution.py:295
  91.6 11.9 %collective-permute-start.6 = (f32[1,96,128]{2,1,0:T(8,128)}, f32[1,96,128]{2,1,0:T(8,128)S(1)}, u32[]{:S(2)}, u32[]{:S(2)}) collective-permute-start(f32[1,96,128]{2,1,0:T(8,128)} %get-tuple-element.13), channel_id=1, source_target_pairs={{0,1},{1,2},{2,3},{3,4},{4,5},{5,6},{6,7},{7,8},{8,9},{9,10},{10,1... | collective-permute-start | bytes 147464 | tf_op jit(solution)/shard_map/ppermute | solution.py:300
  95.0 8.4 %collective-permute-start.7 = (f32[1,96,128]{2,1,0:T(8,128)S(1)}, f32[1,96,128]{2,1,0:T(8,128)S(1)}, u32[]{:S(2)}, u32[]{:S(2)}) collective-permute-start(f32[1,96,128]{2,1,0:T(8,128)S(1)} %copy-done.10), channel_id=1, source_target_pairs={{0,9},{1,10},{2,11},{3,12},{4,13},{5,14},{6,15},{8,1},{9,2},{10,3}... | collective-permute-start | bytes 147464 | tf_op jit(solution)/shard_map/ppermute | solution.py:297
  97.0 6.5 %collective-permute-start.8 = (f32[1,96,128]{2,1,0:T(8,128)}, f32[1,96,128]{2,1,0:T(8,128)S(1)}, u32[]{:S(2)}, u32[]{:S(2)}) collective-permute-start(f32[1,96,128]{2,1,0:T(8,128)} %get-tuple-element.15), channel_id=1, source_target_pairs={{1,0},{2,1},{3,2},{4,3},{5,4},{6,5},{7,6},{8,7},{9,8},{10,9},{11,1... | collective-permute-start | bytes 147464 | tf_op jit(solution)/shard_map/ppermute | solution.py:299
  99.4 8.3 %collective-permute-start.9 = (f32[1,96,128]{2,1,0:T(8,128)S(1)}, f32[1,96,128]{2,1,0:T(8,128)S(1)}, u32[]{:S(2)}, u32[]{:S(2)}) collective-permute-start(f32[1,96,128]{2,1,0:T(8,128)S(1)} %copy-done.9), channel_id=1, source_target_pairs={{0,7},{1,8},{2,9},{3,10},{4,11},{5,12},{6,13},{7,14},{9,0},{10,1},... | collective-permute-start | bytes 147464 | tf_op jit(solution)/shard_map/ppermute | solution.py:296
  103.5 4.2 %copy-start.3 = (f32[1,96,128]{2,1,0:T(8,128)}, f32[1,96,128]{2,1,0:T(8,128)S(1)}, u32[]{:S(2)}) copy-start(f32[1,96,128]{2,1,0:T(8,128)S(1)} %collective-permute-done.6.before_ref) | copy-start | bytes 147460
  103.5 4.2 %copy-start.4 = (f32[1,96,128]{2,1,0:T(8,128)}, f32[1,96,128]{2,1,0:T(8,128)S(1)}, u32[]{:S(2)}) copy-start(f32[1,96,128]{2,1,0:T(8,128)S(1)} %collective-permute-done.7.before_far_ref) | copy-start | bytes 147460
  103.5 4.2 %copy-start.5 = (f32[1,96,128]{2,1,0:T(8,128)}, f32[1,96,128]{2,1,0:T(8,128)S(1)}, u32[]{:S(2)}) copy-start(f32[1,96,128]{2,1,0:T(8,128)S(1)} %collective-permute-done.8.after_ref) | copy-start | bytes 147460
  107.6 0.6 copy-start.6
  107.7 0.7 copy-start.2
